TPU v7x, 32 devices: a whole 2x2x4 slice. The times are simulated.
32 devices in a mesh: groups: 2 (over x), role: 2 (over core), seq: 8 (over z, y).
Axes of the slice: x: 2, y: 2, z: 4, core: 2. Of those that a mesh axis runs over, the one named last changes fastest.
Arguments:
- kv_store: bfloat16 [2, 8192, 1024], P('role', ('groups', 'seq')), parts along dimension 1, may hold values from -6 to 6
- queries: bfloat16 [2, 256, 2, 4096], P('role', ('groups', 'seq')), parts along dimension 1, may hold values from -100 to 100
- step_kv: bfloat16 [256, 2, 1024], P(('groups', 'seq')), parts along dimension 0, may hold values from -6 to 6
- suffix_pages: int32 [256, 2], P(('groups', 'seq')), parts along dimension 0, may hold values from 0 to 31, as said below
- suffix_len: int32 [256], P(('groups', 'seq')), parts along dimension 0, may hold values from 2 to 32, as said below
- owner: int32 [256, 1], P(('groups', 'seq')), parts along dimension 0, may hold values from 0 to 7; in each aligned block of 16 rows (0 to 15, 16 to 31, ...) at most 4 rows name the same one
- parent_id: int32 [256], P(('groups', 'seq')), parts along dimension 0, may hold values from 0 to 1
- parent_pages: int32 [32, 16], P(('groups', 'seq')), parts along dimension 0, may hold values from 0 to 31, as said below
- parent_len: int32 [32], P(('groups', 'seq')), parts along dimension 0, may hold values from 1 to 256, as said below
Outputs:
- served: bfloat16 [2, 256, 2, 4096], P('role', ('groups', 'seq')), parts along dimension 1
There are 2 independent parts, one for each index of `groups`. A program takes and returns all parts, laid end to end along the dimension named above; each array names one. Nothing has to cross between parts.
Inputs may be any that keep to these rules, and one draw needn't show every extreme that they name: `suffix_pages`: on each device the page lists of its 16 requests are disjoint and together name every page of its store once. `suffix_len`: the first request of every device has the full 32 tokens. Of the requests of one device at most 4 go to one owner, and some device sends 4 to one owner. `parent_pages`: on each device the page tables of its 2 parent slots are disjoint and together name every page of its store once. `parent_len`: the first parent slot of every device has the full 256 tokens.
All inputs are finite; a program needn't handle non-finite values.
Results may differ from a plain program's by a relative error of at most 0.0025.
Values may be sent and summed in bfloat16 or wider, within the bound.
A program may use at most 128 MiB of HBM per device.

v0:
```python
import functools

import jax
import jax.numpy as jnp
from jax import lax
from jax.experimental import pallas as pl
from jax.experimental.pallas import tpu as pltpu
from jax.sharding import PartitionSpec as P

HEAD_DIM = 128
KV_HEADS = 4
GROUP = 8
PAGE = 16
LANES = 128

MASKED_SCORE = -1e30
MESH = pl.DeviceIdType.MESH


def iota(shape, dim):
    return lax.broadcasted_iota(jnp.int32, shape, dim)


def spread(index, scalars):
    out = jnp.zeros(index.shape, jnp.int32)
    for i, scalar in enumerate(scalars):
        out = jnp.where(index == i, scalar, out)
    return out


def kernel(
    n_seq,
    cap,
    owner_hbm,
    parent_id_hbm,
    suffix_len_hbm,
    suffix_pages_hbm,
    parent_pages_hbm,
    parent_len_hbm,
    q_hbm,
    kv_hbm,
    step_hbm,
    out_ref,
    owner,
    parent_id,
    suffix_len,
    suffix_pages,
    parent_pages,
    parent_len,
    q_ref,
    kv_ref,
    step_in,
    step_ref,
    slots,
    arrived,
    key_meta,
    slot_bias,
    far_out,
    near_send,
    near_stat_send,
    ret_send,
    ret_stat_send,
    ret,
    ret_stat,
    partner_q,
    partner_o,
    partner_stat,
    load_sem,
    send_sem,
    recv_sem,
    osend_sem,
    orecv_sem,
    ssend_sem,
    srecv_sem,
    psend_sem,
    precv_sem,
):
    role = lax.axis_index("role")
    me = lax.axis_index("seq")
    requests, turns, q_width = q_ref.shape
    tokens = requests * turns
    per_peer = 2 * cap
    slot_rows = n_seq * per_peer
    key_count = kv_ref.shape[0]
    key_width = KV_HEADS * HEAD_DIM
    scale = HEAD_DIM ** (-0.5)
    partner = {"role": 1 - role}
    on_decode = role == 1
    on_prefill = role == 0
    heads_all = KV_HEADS * GROUP
    group_width = GROUP * HEAD_DIM
    half = LANES // 2

    bits = [(me // 2**b) % 2 for b in range(n_seq.bit_length() - 1)]

    def peer_at(step):
        if n_seq & (n_seq - 1):
            return lax.rem(me + step, n_seq)
        peer = me
        for b, mine in enumerate(bits):
            if isinstance(step, int):
                if (step >> b) & 1:
                    peer = peer + 2**b * (1 - 2 * mine)
            else:
                peer = peer + 2**b * (1 - 2 * mine) * ((step // 2**b) % 2)
        return peer

    barrier = pltpu.get_barrier_semaphore()
    @pl.when(on_decode)
    def _():
        for step in range(n_seq - 1, 0, -1):
            pl.semaphore_signal(
                barrier, inc=1, device_id={"seq": peer_at(step)}, device_id_type=MESH
            )

    pl.semaphore_signal(barrier, inc=1, device_id=partner, device_id_type=MESH)

    load_q = pltpu.make_async_copy(q_hbm, q_ref, load_sem.at[0])
    load_step = pltpu.make_async_copy(step_hbm, step_in, load_sem.at[1])
    load_kv = pltpu.make_async_copy(kv_hbm, kv_ref, load_sem.at[2])
    tables = [
        pltpu.make_async_copy(src, dst, load_sem.at[3 + i])
        for i, (src, dst) in enumerate(
            (
                (owner_hbm, owner),
                (parent_id_hbm, parent_id),
                (suffix_len_hbm, suffix_len),
                (suffix_pages_hbm, suffix_pages),
                (parent_pages_hbm, parent_pages),
                (parent_len_hbm, parent_len),
            )
        )
    ]
    load_q.start()
    for table in tables:
        table.start()
    load_step.start()
    load_kv.start()

    def remote(src, dst, ssem, rsem, device):
        return pltpu.make_async_remote_copy(
            src_ref=src,
            dst_ref=dst,
            send_sem=ssem,
            recv_sem=rsem,
            device_id=device,
            device_id_type=MESH,
        )

    q_to_partner = remote(q_ref, partner_q, psend_sem.at[0], precv_sem.at[0], partner)
    o_to_partner = remote(near_send, partner_o, psend_sem.at[1], precv_sem.at[1], partner)
    s_to_partner = remote(near_stat_send, partner_stat, psend_sem.at[2], precv_sem.at[2], partner)

    def q_lanes(g):
        first = 0 if g == 0 else LANES + g * group_width
        return slice(first, LANES + (g + 1) * group_width)

    def slots_to(peer, mine, g):
        return remote(
            slots.at[peer, :, q_lanes(g)],
            arrived.at[mine, :, q_lanes(g)],
            send_sem.at[peer, g],
            recv_sem.at[mine, g],
            {"seq": peer},
        )

    def out_to(peer, mine, g):
        lanes = slice(g * group_width, (g + 1) * group_width)
        return remote(
            ret_send.at[peer, :, lanes],
            ret.at[mine, :, lanes],
            osend_sem.at[peer, g],
            orecv_sem.at[mine, g],
            {"seq": peer},
        )

    def stat_to(peer, mine):
        return remote(
            ret_stat_send.at[peer],
            ret_stat.at[mine],
            ssend_sem.at[peer],
            srecv_sem.at[mine],
            {"seq": peer},
        )

    for table in tables:
        table.wait()
    owners = [owner[r] for r in range(requests)]
    places = []
    for r in range(requests):
        rank = jnp.int32(0)
        for e in range(r):
            rank = rank + jnp.where(owners[e] == owners[r], 1, 0)
        places.append(owners[r] * cap + rank)
    lengths = [suffix_len[r] for r in range(requests)]
    parents = [parent_id[r] for r in range(requests)]

    load_q.wait()

    @pl.when(on_decode)
    def _():
        col = iota((1, tokens), 1)
        target = 2 * spread(col >> 1, places) + (col & 1)
        pick = jnp.where(iota((slot_rows, tokens), 0) == target, 1.0, 0.0).astype(jnp.bfloat16)
        tok = iota((tokens, LANES), 0) >> 1
        pid = spread(tok, parents).astype(jnp.float32).astype(jnp.bfloat16)
        pid_slots = jnp.dot(pick, pid, preferred_element_type=jnp.float32)
        for d in range(n_seq):
            slots[d, :, :LANES] = pid_slots[d * per_peer : (d + 1) * per_peer].astype(
                jnp.bfloat16
            )
        block = 4 * LANES
        for c in range(q_width // block):
            lanes = slice(c * block, (c + 1) * block)
            part = jnp.dot(
                pick, q_ref[:, :, lanes].reshape(tokens, block), preferred_element_type=jnp.float32
            )
            for d in range(n_seq):
                slots[d, :, LANES + c * block : LANES + (c + 1) * block] = part[d * per_peer : (d + 1) * per_peer].astype(jnp.bfloat16)
        pl.semaphore_wait(barrier, n_seq)
        q_to_partner.start()
        for g in range(KV_HEADS):
            for step in range(n_seq - 1, 0, -1):
                slots_to(peer_at(step), me, g).start()
        arrived[pl.ds(me, 1)] = slots[pl.ds(me, 1)]

    @pl.when(on_prefill)
    def _():
        pl.semaphore_wait(barrier, 1)

    lane_page = iota((1, key_count), 1) // PAGE
    group_row = jnp.zeros((1, key_count), jnp.int32)
    base_row = jnp.zeros((1, key_count), jnp.int32)
    suf_pages = suffix_pages.shape[0]
    par_pages = parent_pages.shape[1]
    for j in range(key_count // PAGE):
        page = jnp.where(
            on_prefill,
            suffix_pages[j % suf_pages, j // suf_pages],
            parent_pages[j // par_pages, j % par_pages],
        )
        here = lane_page == page
        group_row = jnp.where(here, jnp.where(on_prefill, j // suf_pages, j // par_pages), group_row)
        base_row = jnp.where(
            here, jnp.where(on_prefill, j % suf_pages, j % par_pages) * PAGE, base_row
        )
    pos_row = base_row + (iota((1, key_count), 1) & (PAGE - 1))
    key_meta[0:1, :] = group_row
    key_meta[1:2, :] = pos_row
    load_step.wait()
    for c in range(step_ref.shape[1] // (4 * LANES)):
        lanes = slice(c * 4 * LANES, (c + 1) * 4 * LANES)
        step_ref[:, lanes] = step_in[:, :, lanes].reshape(tokens, 4 * LANES)
    cuts = [parent_len[a] for a in range(parent_len.shape[0])]
    load_kv.wait()

    def bias_of(group, limit):
        keep = (key_meta[0:1, :] == group) & (key_meta[1:2, :] < limit)
        return jnp.where(keep, 0.0, MASKED_SCORE)

    def attend(g, query, bias, step_bias=None):
        rows = bias.shape[0]
        ks = slice(g * HEAD_DIM, (g + 1) * HEAD_DIM)
        vs = slice(key_width + g * HEAD_DIM, key_width + (g + 1) * HEAD_DIM)
        contract = (((1,), (1,)), ((), ()))

        def scores(keys, add):
            found = lax.dot_general(query, keys, contract, preferred_element_type=jnp.float32)
            return found.reshape(GROUP, rows, keys.shape[0]) * scale + add[None]

        def blend(term, values):
            term = term.reshape(GROUP * rows, values.shape[0]).astype(jnp.bfloat16)
            mixed = jnp.dot(term, values, preferred_element_type=jnp.float32)
            return mixed.reshape(GROUP, rows, HEAD_DIM)

        score = scores(kv_ref[:, ks], bias)
        top = jnp.max(score, axis=2, keepdims=True)
        if step_bias is not None:
            step_score = scores(step_ref[:, ks], step_bias)
            top = jnp.maximum(top, jnp.max(step_score, axis=2, keepdims=True))
        term = jnp.exp(score - top)
        total = jnp.sum(term, axis=2, keepdims=True)
        mixed = blend(term, kv_ref[:, vs])
        if step_bias is not None:
            step_term = jnp.exp(step_score - top)
            total = total + jnp.sum(step_term, axis=2, keepdims=True)
            mixed = mixed + blend(step_term, step_ref[:, vs])
        return mixed / total, top, total

    def record(g, top, total):
        lane = iota((top.shape[1], LANES), 1)
        stat = jnp.zeros(lane.shape, jnp.float32)
        for h in range(GROUP):
            stat = jnp.where(lane == g * GROUP + h, top[h], stat)
            stat = jnp.where(lane == half + g * GROUP + h, total[h], stat)
        return stat

    def swapped(stat):
        return jnp.concatenate([stat[:, half:], stat[:, :half]], axis=1)

    @pl.when(on_prefill)
    def _():
        row = iota((tokens, 1), 0)
        request = row >> 1
        turn = row & 1
        length = spread(request, lengths)

        def lanes_of(head):
            return slice(head * HEAD_DIM, (head + 1) * HEAD_DIM)

        def own(head):
            return q_ref[:, :, lanes_of(head)].reshape(tokens, HEAD_DIM)

        def passed(head):
            return partner_q[:, :, lanes_of(head)].reshape(tokens, HEAD_DIM)

        def serve(head, value):
            out_ref[:, lanes_of(head)] = value.astype(jnp.bfloat16)

        def keep(head, value):
            near_send[:, lanes_of(head)] = value

        q_to_partner.wait_recv()
        bias = bias_of(request, length)
        step_key = iota((tokens, tokens), 1)
        step_keep = ((step_key >> 1) == request) & ((step_key & 1) < turn + 1)
        step_bias = jnp.where(step_keep, 0.0, MASKED_SCORE)
        stat = jnp.zeros((tokens, LANES), jnp.float32)
        for g in range(KV_HEADS):
            heads = range(g * GROUP, (g + 1) * GROUP)
            query = jnp.concatenate([passed(head) for head in heads], axis=0)
            mixed, top, total = attend(g, query, bias, step_bias)
            for h, head in enumerate(heads):
                keep(head, mixed[h])
            stat = stat + record(g, top, total)
        near_stat_send[...] = stat
        o_to_partner.start()
        s_to_partner.start()
        bias = bias_of(request, length - 1 + turn)
        for g in range(KV_HEADS):
            heads = range(g * GROUP, (g + 1) * GROUP)
            query = jnp.concatenate([own(head) for head in heads], axis=0)
            mixed, _, _ = attend(g, query, bias)
            for h, head in enumerate(heads):
                serve(head, mixed[h])
        s_to_partner.wait_send()
        o_to_partner.wait_send()

    batch = min(8, n_seq)

    def answer(c, g, batch):
        batch_rows = batch * per_peer
        steps = [n_seq - 1 - batch * c - i for i in range(batch)]
        peers = [peer_at(step) for step in steps]

        def unless_own(step, action):
            if isinstance(step, int):
                if step > 0:
                    action()
            else:
                pl.when(step > 0)(action)

        for step, peer in zip(steps, peers):
            unless_own(step, lambda peer=peer: slots_to(me, peer, g).wait_recv())

        def gathered(first):
            return jnp.concatenate(
                [arrived[peer, :, first : first + LANES].astype(jnp.float32) for peer in peers],
                axis=0,
            )

        rows = pl.ds(c * batch_rows, batch_rows)
        if g == 0:
            group = gathered(0).astype(jnp.int32)[:, 0:1]
            slot_bias[rows, :] = bias_of(group, spread(group, cuts))
        query = jnp.concatenate(
            [
                gathered(LANES + head * HEAD_DIM).astype(jnp.bfloat16)
                for head in range(g * GROUP, (g + 1) * GROUP)
            ],
            axis=0,
        )
        mixed, top, total = attend(g, query, slot_bias[rows, :])
        for h in range(GROUP):
            head = g * GROUP + h
            for i, peer in enumerate(peers):
                ret_send[peer, :, head * HEAD_DIM : (head + 1) * HEAD_DIM] = mixed[
                    h, i * per_peer : (i + 1) * per_peer
                ].astype(jnp.bfloat16)
        stat = record(g, top, total)
        for i, peer in enumerate(peers):
            part = stat[i * per_peer : (i + 1) * per_peer]
            ret_stat_send[peer] = part if g == 0 else ret_stat_send[peer] + part

        def reply(peer):
            if g == KV_HEADS - 1:
                stat_to(peer, me).start()
            out_to(peer, me, g).start()

        for step, peer in zip(steps, peers):
            unless_own(step, lambda peer=peer: reply(peer))

    @pl.when(on_decode)
    def _():
        for g in range(KV_HEADS):
            if n_seq == batch:
                pieces = 2 if g == KV_HEADS - 1 and batch % 2 == 0 else 1
                for c in range(pieces):
                    answer(c, g, batch // pieces)
            else:

                def one(c, carry):
                    answer(c, g, batch)
                    return carry

                lax.fori_loop(0, n_seq // batch, one, 0)

    @pl.when(on_decode)
    def _():
        ret[pl.ds(me, 1)] = ret_send[pl.ds(me, 1)]
        ret_stat[pl.ds(me, 1)] = ret_stat_send[pl.ds(me, 1)]
        tok = iota((tokens, 1), 0)
        target = 2 * spread(tok >> 1, places) + (tok & 1)
        unpick = jnp.where(iota((tokens, slot_rows), 1) == target, 1.0, 0.0)
        o_to_partner.wait_recv()
        s_to_partner.wait_recv()
        pick_back = unpick.astype(jnp.bfloat16)
        for g in range(KV_HEADS):
            for step in range(n_seq - 1, 0, -1):
                out_to(me, peer_at(step), g).wait_recv()
            for head in range(g * GROUP, (g + 1) * GROUP):
                part = slice(head * HEAD_DIM, (head + 1) * HEAD_DIM)
                came = jnp.concatenate(
                    [ret[s, :, part].astype(jnp.float32) for s in range(n_seq)], axis=0
                ).astype(jnp.bfloat16)
                far_out[:, part] = jnp.dot(pick_back, came, preferred_element_type=jnp.float32)
        for step in range(n_seq - 1, 0, -1):
            stat_to(me, peer_at(step)).wait_recv()
        back = jnp.concatenate([ret_stat[s] for s in range(n_seq)], axis=0)
        far_top = jnp.dot(
            unpick, back, preferred_element_type=jnp.float32, precision=lax.Precision.HIGHEST
        )
        far_sum = swapped(far_top)
        near_top = partner_stat[...]
        near_sum = swapped(near_top)
        top = jnp.maximum(far_top, near_top)
        far_weight = far_sum * jnp.exp(far_top - top)
        near_weight = near_sum * jnp.exp(near_top - top)
        total = jnp.where(near_weight + far_weight == 0.0, 1.0, near_weight + far_weight)
        far_share = far_weight / total
        for head in range(heads_all):
            part = slice(head * HEAD_DIM, (head + 1) * HEAD_DIM)
            near = partner_o[:, part]
            out_ref[:, part] = (
                near + (far_out[:, part] - near) * far_share[:, head : head + 1]
            ).astype(jnp.bfloat16)
        q_to_partner.wait_send()
        for step in range(1, n_seq):
            peer = peer_at(step)
            for g in range(KV_HEADS):
                slots_to(peer, me, g).wait_send()
                out_to(peer, me, g).wait_send()
            stat_to(peer, me).wait_send()


def local(
    kv_store, queries, step_kv, suffix_pages, suffix_len, owner, parent_id, parent_pages, parent_len
):
    n_seq = lax.axis_size("seq")
    page_store = kv_store[0]
    requests, turns, q_width = queries.shape[1:]
    tokens = requests * turns
    cap = max(4, 2 * requests // n_seq)
    per_peer = 2 * cap
    bf16, f32 = jnp.bfloat16, jnp.float32
    vmem = pl.BlockSpec(memory_space=pltpu.VMEM)
    hbm = pl.BlockSpec(memory_space=pl.ANY)
    dma = pltpu.SemaphoreType.DMA
    served = pl.pallas_call(
        functools.partial(kernel, n_seq, cap),
        out_shape=pltpu.VMEM((tokens, q_width), bf16),
        in_specs=[hbm] * 9,
        out_specs=vmem,
        scratch_shapes=[
            pltpu.SMEM((requests,), jnp.int32),
            pltpu.SMEM((requests,), jnp.int32),
            pltpu.SMEM((requests,), jnp.int32),
            pltpu.SMEM(suffix_pages.shape[::-1], jnp.int32),
            pltpu.SMEM(parent_pages.shape, jnp.int32),
            pltpu.SMEM(parent_len.shape, jnp.int32),
            pltpu.VMEM((requests, turns, q_width), bf16),
            pltpu.VMEM(page_store.shape, bf16),
            pltpu.VMEM(step_kv.shape, bf16),
            pltpu.VMEM((tokens, step_kv.shape[2]), bf16),
            pltpu.VMEM((n_seq, per_peer, q_width + LANES), bf16),
            pltpu.VMEM((n_seq, per_peer, q_width + LANES), bf16),
            pltpu.VMEM((8, page_store.shape[0]), jnp.int32),
            pltpu.VMEM((n_seq * per_peer, page_store.shape[0]), f32),
            pltpu.VMEM((tokens, q_width), f32),
            pltpu.VMEM((tokens, q_width), f32),
            pltpu.VMEM((tokens, LANES), f32),
            pltpu.VMEM((n_seq, per_peer, q_width), bf16),
            pltpu.VMEM((n_seq, per_peer, LANES), f32),
            pltpu.VMEM((n_seq, per_peer, q_width), bf16),
            pltpu.VMEM((n_seq, per_peer, LANES), f32),
            pltpu.VMEM((requests, turns, q_width), bf16),
            pltpu.VMEM((tokens, q_width), f32),
            pltpu.VMEM((tokens, LANES), f32),
            dma((9,)),
            dma((n_seq, KV_HEADS)),
            dma((n_seq, KV_HEADS)),
            dma((n_seq, KV_HEADS)),
            dma((n_seq, KV_HEADS)),
            dma((n_seq,)),
            dma((n_seq,)),
            dma((3,)),
            dma((3,)),
        ],
        compiler_params=pltpu.CompilerParams(
            collective_id=0, has_side_effects=True, vmem_limit_bytes=60 * 1024 * 1024
        ),
    )(
        owner.reshape(-1),
        parent_id,
        suffix_len,
        suffix_pages.T,
        parent_pages,
        parent_len,
        queries[0],
        page_store,
        step_kv,
    )
    return served.reshape(1, requests, turns, q_width)


def solution(mesh):
    in_specs = (
        P("role", ("groups", "seq"), None),
        P("role", ("groups", "seq"), None, None),
        P(("groups", "seq"), None, None),
        P(("groups", "seq"), None),
        P(("groups", "seq")),
        P(("groups", "seq"), None),
        P(("groups", "seq")),
        P(("groups", "seq"), None),
        P(("groups", "seq")),
    )
    out_specs = P("role", ("groups", "seq"), None, None)
    return jax.shard_map(local, mesh=mesh, in_specs=in_specs, out_specs=out_specs, check_vma=False)
```

profile of v0, /device:TPU:1, one launch (start us, length us, event | category | flops | bytes accessed | tf_op | source)
XLA Modules:
  0.0 21.2 jit_solution(12656502702019407433)
XLA Ops:
  0.0 20.3 %shard_map.91 = bf16[32,4096]{1,0:T(8,128)(2,1)S(1)} custom-call(s32[16]{0:T(128)} %bitcast.7, s32[16]{0:T(128)} %parent_id_hbm.1, s32[16]{0:T(128)} %suffix_len_hbm.1, s32[2,16]{1,0:T(2,128)} %bitcast.6, s32[2,16]{1,0:T(2,128)} %parent_pages_hbm.1, s32[2]{0:T(128)} %parent_len_hbm.1, bf16[16,2,4096]{2,1,0:T(2,128)(2,1)} %bitcast.5, ...), custom_call_target="tpu_custom_call" | custom-call | tf_op jit(solution)/shard_map/pallas_call | solution.py:479
  20.3 0.9 %reshape.7 = bf16[1,16,2,4096]{3,2,1,0:T(2,128)(2,1)} reshape(bf16[32,4096]{1,0:T(8,128)(2,1)S(1)} %shard_map.91) | data formatting | bytes 524288 | tf_op jit(solution)/shard_map/reshape | solution.py:533
where the time goes:
time: 21.3 us; the launch traced here: 21.2 us
  Pallas kernels  20.3 us (95%)
  local copies, waits for them, and re-layouts  0.89 us (4%)
    pallas_call x1, Pallas kernels, local(): pl.pallas_call(functools.partial(kernel, n_seq, cap), out_shape=pltpu.VME...  20.3 us
    reshape x1, local copies, waits for them, and re-layouts, local(): return served.reshape(1, requests, turns, q_width)  0.89 us

commit v1 on v0

--- a/solution.py
+++ b/solution.py
@@ -55,23 +55,19 @@
     arrived,
     key_meta,
     slot_bias,
+    slot_stat,
     far_out,
     near_send,
     near_stat_send,
     ret_send,
-    ret_stat_send,
     ret,
-    ret_stat,
     partner_q,
     partner_o,
     partner_stat,
     load_sem,
     send_sem,
     recv_sem,
-    osend_sem,
     orecv_sem,
-    ssend_sem,
-    srecv_sem,
     psend_sem,
     precv_sem,
 ):
@@ -90,12 +86,10 @@
     heads_all = KV_HEADS * GROUP
     group_width = GROUP * HEAD_DIM
     half = LANES // 2
-
+    unit = min(4, n_seq)
     bits = [(me // 2**b) % 2 for b in range(n_seq.bit_length() - 1)]
 
     def peer_at(step):
-        if n_seq & (n_seq - 1):
-            return lax.rem(me + step, n_seq)
         peer = me
         for b, mine in enumerate(bits):
             if isinstance(step, int):
@@ -105,21 +99,27 @@
                 peer = peer + 2**b * (1 - 2 * mine) * ((step // 2**b) % 2)
         return peer
 
+    def each(first, last, action):
+        def body(i, carry):
+            action(i)
+            return carry
+
+        lax.fori_loop(first, last, body, 0)
+
     barrier = pltpu.get_barrier_semaphore()
+
+    def greet(peer):
+        pl.semaphore_signal(barrier, inc=1, device_id={"seq": peer}, device_id_type=MESH)
+
+    pl.semaphore_signal(barrier, inc=1, device_id=partner, device_id_type=MESH)
+
     @pl.when(on_decode)
     def _():
         for step in range(n_seq - 1, 0, -1):
-            pl.semaphore_signal(
-                barrier, inc=1, device_id={"seq": peer_at(step)}, device_id_type=MESH
-            )
-
-    pl.semaphore_signal(barrier, inc=1, device_id=partner, device_id_type=MESH)
-
-    load_q = pltpu.make_async_copy(q_hbm, q_ref, load_sem.at[0])
-    load_step = pltpu.make_async_copy(step_hbm, step_in, load_sem.at[1])
-    load_kv = pltpu.make_async_copy(kv_hbm, kv_ref, load_sem.at[2])
+            greet(peer_at(step))
+
     tables = [
-        pltpu.make_async_copy(src, dst, load_sem.at[3 + i])
+        pltpu.make_async_copy(src, dst, load_sem.at[i])
         for i, (src, dst) in enumerate(
             (
                 (owner_hbm, owner),
@@ -131,11 +131,26 @@
             )
         )
     ]
-    load_q.start()
-    for table in tables:
+    load_step = pltpu.make_async_copy(step_hbm, step_in, load_sem.at[6])
+    load_kv = pltpu.make_async_copy(kv_hbm, kv_ref, load_sem.at[7])
+
+    def out_lanes(g):
+        return slice(g * group_width, (g + 1) * group_width)
+
+    load_q = [
+        pltpu.make_async_copy(
+            q_hbm.at[:, :, out_lanes(g)], q_ref.at[:, :, out_lanes(g)], load_sem.at[8 + g]
+        )
+        for g in range(KV_HEADS)
+    ]
+    for table in tables[:2]:
         table.start()
+    for part in load_q:
+        part.start()
+    for table in tables[2:]:
+        table.start()
+    load_kv.start()
     load_step.start()
-    load_kv.start()
 
     def remote(src, dst, ssem, rsem, device):
         return pltpu.make_async_remote_copy(
@@ -155,35 +170,50 @@
         first = 0 if g == 0 else LANES + g * group_width
         return slice(first, LANES + (g + 1) * group_width)
 
-    def slots_to(peer, mine, g):
+    def ret_lanes(g):
+        last = LANES if g == KV_HEADS - 1 else 0
+        return slice(g * group_width, (g + 1) * group_width + last)
+
+    def slots_to(step, g):
+        peer = peer_at(step)
         return remote(
             slots.at[peer, :, q_lanes(g)],
-            arrived.at[mine, :, q_lanes(g)],
-            send_sem.at[peer, g],
-            recv_sem.at[mine, g],
+            arrived.at[me, :, q_lanes(g)],
+            send_sem.at[0],
+            recv_sem.at[step // unit, g],
             {"seq": peer},
         )
 
-    def out_to(peer, mine, g):
-        lanes = slice(g * group_width, (g + 1) * group_width)
+    def slots_from(u, g, count):
+        rows = pl.ds(0, count)
         return remote(
-            ret_send.at[peer, :, lanes],
-            ret.at[mine, :, lanes],
-            osend_sem.at[peer, g],
-            orecv_sem.at[mine, g],
+            slots.at[rows, :, q_lanes(g)],
+            arrived.at[rows, :, q_lanes(g)],
+            send_sem.at[0],
+            recv_sem.at[u, g],
+            {"seq": me},
+        )
+
+    def out_to(peer, g):
+        return remote(
+            ret_send.at[peer, :, ret_lanes(g)],
+            ret.at[me, :, ret_lanes(g)],
+            send_sem.at[1],
+            orecv_sem.at[g],
             {"seq": peer},
         )
 
-    def stat_to(peer, mine):
+    def out_from(g):
+        rows = pl.ds(0, n_seq - 1)
         return remote(
-            ret_stat_send.at[peer],
-            ret_stat.at[mine],
-            ssend_sem.at[peer],
-            srecv_sem.at[mine],
-            {"seq": peer},
-        )
-
-    for table in tables:
+            ret_send.at[rows, :, ret_lanes(g)],
+            ret.at[rows, :, ret_lanes(g)],
+            send_sem.at[1],
+            orecv_sem.at[g],
+            {"seq": me},
+        )
+
+    for table in tables[:2]:
         table.wait()
     owners = [owner[r] for r in range(requests)]
     places = []
@@ -192,10 +222,7 @@
         for e in range(r):
             rank = rank + jnp.where(owners[e] == owners[r], 1, 0)
         places.append(owners[r] * cap + rank)
-    lengths = [suffix_len[r] for r in range(requests)]
     parents = [parent_id[r] for r in range(requests)]
-
-    load_q.wait()
 
     @pl.when(on_decode)
     def _():
@@ -209,25 +236,36 @@
             slots[d, :, :LANES] = pid_slots[d * per_peer : (d + 1) * per_peer].astype(
                 jnp.bfloat16
             )
-        block = 4 * LANES
-        for c in range(q_width // block):
-            lanes = slice(c * block, (c + 1) * block)
-            part = jnp.dot(
-                pick, q_ref[:, :, lanes].reshape(tokens, block), preferred_element_type=jnp.float32
-            )
-            for d in range(n_seq):
-                slots[d, :, LANES + c * block : LANES + (c + 1) * block] = part[d * per_peer : (d + 1) * per_peer].astype(jnp.bfloat16)
-        pl.semaphore_wait(barrier, n_seq)
+        block_lanes = 4 * LANES
+        for g in range(KV_HEADS):
+            load_q[g].wait()
+            for c in range(group_width // block_lanes):
+                first = g * group_width + c * block_lanes
+                part = jnp.dot(
+                    pick,
+                    q_ref[:, :, first : first + block_lanes].reshape(tokens, block_lanes),
+                    preferred_element_type=jnp.float32,
+                )
+                for d in range(n_seq):
+                    slots[d, :, LANES + first : LANES + first + block_lanes] = part[
+                        d * per_peer : (d + 1) * per_peer
+                    ].astype(jnp.bfloat16)
+            if g == 0:
+                pl.semaphore_wait(barrier, n_seq)
+            for step in range(n_seq - 1, 0, -1):
+                slots_to(step, g).start()
         q_to_partner.start()
-        for g in range(KV_HEADS):
-            for step in range(n_seq - 1, 0, -1):
-                slots_to(peer_at(step), me, g).start()
         arrived[pl.ds(me, 1)] = slots[pl.ds(me, 1)]
 
     @pl.when(on_prefill)
     def _():
         pl.semaphore_wait(barrier, 1)
-
+        for part in load_q:
+            part.wait()
+
+    for table in tables[2:]:
+        table.wait()
+    lengths = [suffix_len[r] for r in range(requests)]
     lane_page = iota((1, key_count), 1) // PAGE
     group_row = jnp.zeros((1, key_count), jnp.int32)
     base_row = jnp.zeros((1, key_count), jnp.int32)
@@ -247,10 +285,15 @@
     pos_row = base_row + (iota((1, key_count), 1) & (PAGE - 1))
     key_meta[0:1, :] = group_row
     key_meta[1:2, :] = pos_row
+
     load_step.wait()
-    for c in range(step_ref.shape[1] // (4 * LANES)):
-        lanes = slice(c * 4 * LANES, (c + 1) * 4 * LANES)
-        step_ref[:, lanes] = step_in[:, :, lanes].reshape(tokens, 4 * LANES)
+
+    @pl.when(on_prefill)
+    def _():
+        for c in range(step_ref.shape[1] // (4 * LANES)):
+            lanes = slice(c * 4 * LANES, (c + 1) * 4 * LANES)
+            step_ref[:, lanes] = step_in[:, :, lanes].reshape(tokens, 4 * LANES)
+
     cuts = [parent_len[a] for a in range(parent_len.shape[0])]
     load_kv.wait()
 
@@ -295,8 +338,10 @@
             stat = jnp.where(lane == half + g * GROUP + h, total[h], stat)
         return stat
 
-    def swapped(stat):
-        return jnp.concatenate([stat[:, half:], stat[:, :half]], axis=1)
+    def log_sum(stat):
+        lane = iota(stat.shape, 1)
+        total = jnp.where(lane < heads_all, pltpu.roll(stat, half, 1), 1.0)
+        return jnp.where(lane < heads_all, stat, 0.0) + jnp.log(total)
 
     @pl.when(on_prefill)
     def _():
@@ -333,7 +378,7 @@
             for h, head in enumerate(heads):
                 keep(head, mixed[h])
             stat = stat + record(g, top, total)
-        near_stat_send[...] = stat
+        near_stat_send[...] = log_sum(stat)
         o_to_partner.start()
         s_to_partner.start()
         bias = bias_of(request, length - 1 + turn)
@@ -352,24 +397,22 @@
         batch_rows = batch * per_peer
         steps = [n_seq - 1 - batch * c - i for i in range(batch)]
         peers = [peer_at(step) for step in steps]
-
-        def unless_own(step, action):
-            if isinstance(step, int):
-                if step > 0:
-                    action()
+        rows = pl.ds(c * batch_rows, batch_rows)
+        for step in steps[::unit]:
+            if not isinstance(step, int):
+                pl.when(step // unit > 0)(lambda: slots_from(step // unit, g, unit).wait_recv())
+                pl.when(step // unit == 0)(lambda: slots_from(0, g, unit - 1).wait_recv())
             else:
-                pl.when(step > 0)(action)
-
-        for step, peer in zip(steps, peers):
-            unless_own(step, lambda peer=peer: slots_to(me, peer, g).wait_recv())
+                slots_from(step // unit, g, unit if step >= unit else unit - 1).wait_recv()
 
         def gathered(first):
             return jnp.concatenate(
-                [arrived[peer, :, first : first + LANES].astype(jnp.float32) for peer in peers],
+                [
+                    arrived[peer, :, first : first + LANES].astype(jnp.float32) for peer in peers
+                ],
                 axis=0,
             )
 
-        rows = pl.ds(c * batch_rows, batch_rows)
         if g == 0:
             group = gathered(0).astype(jnp.int32)[:, 0:1]
             slot_bias[rows, :] = bias_of(group, spread(group, cuts))
@@ -388,79 +431,93 @@
                     h, i * per_peer : (i + 1) * per_peer
                 ].astype(jnp.bfloat16)
         stat = record(g, top, total)
-        for i, peer in enumerate(peers):
-            part = stat[i * per_peer : (i + 1) * per_peer]
-            ret_stat_send[peer] = part if g == 0 else ret_stat_send[peer] + part
-
-        def reply(peer):
-            if g == KV_HEADS - 1:
-                stat_to(peer, me).start()
-            out_to(peer, me, g).start()
+        if g > 0:
+            stat = stat + slot_stat[rows, :]
+        if g < KV_HEADS - 1:
+            slot_stat[rows, :] = stat
+        else:
+            value = log_sum(stat)
+            high = value.astype(jnp.bfloat16).astype(jnp.float32)
+            rest = value - high
+            middle = rest.astype(jnp.bfloat16).astype(jnp.float32)
+            low = rest - middle
+            lane = iota(value.shape, 1)
+            packed = jnp.where(
+                lane < heads_all,
+                high,
+                jnp.where(
+                    lane < 2 * heads_all,
+                    pltpu.roll(middle, heads_all, 1),
+                    pltpu.roll(low, 2 * heads_all, 1),
+                ),
+            )
+            for i, peer in enumerate(peers):
+                ret_send[peer, :, q_width:] = packed[
+                    i * per_peer : (i + 1) * per_peer
+                ].astype(jnp.bfloat16)
 
         for step, peer in zip(steps, peers):
-            unless_own(step, lambda peer=peer: reply(peer))
+            if isinstance(step, int):
+                if step > 0:
+                    out_to(peer, g).start()
+            else:
+                pl.when(step > 0)(lambda peer=peer: out_to(peer, g).start())
 
     @pl.when(on_decode)
     def _():
         for g in range(KV_HEADS):
             if n_seq == batch:
-                pieces = 2 if g == KV_HEADS - 1 and batch % 2 == 0 else 1
+                pieces = (1, 1, 1, 2)[g] if batch % 2 == 0 else 1
                 for c in range(pieces):
                     answer(c, g, batch // pieces)
             else:
-
-                def one(c, carry):
-                    answer(c, g, batch)
-                    return carry
-
-                lax.fori_loop(0, n_seq // batch, one, 0)
+                each(0, n_seq // batch, lambda c: answer(c, g, batch))
 
     @pl.when(on_decode)
     def _():
         ret[pl.ds(me, 1)] = ret_send[pl.ds(me, 1)]
-        ret_stat[pl.ds(me, 1)] = ret_stat_send[pl.ds(me, 1)]
         tok = iota((tokens, 1), 0)
         target = 2 * spread(tok >> 1, places) + (tok & 1)
         unpick = jnp.where(iota((tokens, slot_rows), 1) == target, 1.0, 0.0)
         o_to_partner.wait_recv()
         s_to_partner.wait_recv()
         pick_back = unpick.astype(jnp.bfloat16)
+
+        def came(first):
+            rows = jnp.concatenate(
+                [ret[s, :, first : first + LANES].astype(jnp.float32) for s in range(n_seq)],
+                axis=0,
+            ).astype(jnp.bfloat16)
+            return jnp.dot(pick_back, rows, preferred_element_type=jnp.float32)
+
         for g in range(KV_HEADS):
-            for step in range(n_seq - 1, 0, -1):
-                out_to(me, peer_at(step), g).wait_recv()
+            out_from(g).wait_recv()
             for head in range(g * GROUP, (g + 1) * GROUP):
-                part = slice(head * HEAD_DIM, (head + 1) * HEAD_DIM)
-                came = jnp.concatenate(
-                    [ret[s, :, part].astype(jnp.float32) for s in range(n_seq)], axis=0
-                ).astype(jnp.bfloat16)
-                far_out[:, part] = jnp.dot(pick_back, came, preferred_element_type=jnp.float32)
-        for step in range(n_seq - 1, 0, -1):
-            stat_to(me, peer_at(step)).wait_recv()
-        back = jnp.concatenate([ret_stat[s] for s in range(n_seq)], axis=0)
-        far_top = jnp.dot(
-            unpick, back, preferred_element_type=jnp.float32, precision=lax.Precision.HIGHEST
-        )
-        far_sum = swapped(far_top)
-        near_top = partner_stat[...]
-        near_sum = swapped(near_top)
-        top = jnp.maximum(far_top, near_top)
-        far_weight = far_sum * jnp.exp(far_top - top)
-        near_weight = near_sum * jnp.exp(near_top - top)
-        total = jnp.where(near_weight + far_weight == 0.0, 1.0, near_weight + far_weight)
-        far_share = far_weight / total
+                far_out[:, head * HEAD_DIM : (head + 1) * HEAD_DIM] = came(head * HEAD_DIM)
+        parts = came(q_width)
+        far = (
+            parts
+            + pltpu.roll(parts, LANES - heads_all, 1)
+            + pltpu.roll(parts, LANES - 2 * heads_all, 1)
+        )
+        near = partner_stat[...]
+        top = jnp.maximum(far, near)
+        far_weight = jnp.exp(far - top)
+        far_share = far_weight / (far_weight + jnp.exp(near - top))
         for head in range(heads_all):
             part = slice(head * HEAD_DIM, (head + 1) * HEAD_DIM)
-            near = partner_o[:, part]
+            close = partner_o[:, part]
             out_ref[:, part] = (
-                near + (far_out[:, part] - near) * far_share[:, head : head + 1]
+                close + (far_out[:, part] - close) * far_share[:, head : head + 1]
             ).astype(jnp.bfloat16)
         q_to_partner.wait_send()
-        for step in range(1, n_seq):
-            peer = peer_at(step)
-            for g in range(KV_HEADS):
-                slots_to(peer, me, g).wait_send()
-                out_to(peer, me, g).wait_send()
-            stat_to(peer, me).wait_send()
+        rows = pl.ds(0, n_seq - 1)
+        remote(
+            slots.at[rows], arrived.at[rows], send_sem.at[0], recv_sem.at[0, 0], {"seq": me}
+        ).wait_send()
+        remote(
+            ret_send.at[rows], ret.at[rows], send_sem.at[1], orecv_sem.at[0], {"seq": me}
+        ).wait_send()
 
 
 def local(
@@ -472,6 +529,7 @@
     tokens = requests * turns
     cap = max(4, 2 * requests // n_seq)
     per_peer = 2 * cap
+    units = n_seq // min(4, n_seq)
     bf16, f32 = jnp.bfloat16, jnp.float32
     vmem = pl.BlockSpec(memory_space=pltpu.VMEM)
     hbm = pl.BlockSpec(memory_space=pl.ANY)
@@ -496,23 +554,19 @@
             pltpu.VMEM((n_seq, per_peer, q_width + LANES), bf16),
             pltpu.VMEM((8, page_store.shape[0]), jnp.int32),
             pltpu.VMEM((n_seq * per_peer, page_store.shape[0]), f32),
+            pltpu.VMEM((n_seq * per_peer, LANES), f32),
             pltpu.VMEM((tokens, q_width), f32),
             pltpu.VMEM((tokens, q_width), f32),
             pltpu.VMEM((tokens, LANES), f32),
-            pltpu.VMEM((n_seq, per_peer, q_width), bf16),
-            pltpu.VMEM((n_seq, per_peer, LANES), f32),
-            pltpu.VMEM((n_seq, per_peer, q_width), bf16),
-            pltpu.VMEM((n_seq, per_peer, LANES), f32),
+            pltpu.VMEM((n_seq, per_peer, q_width + LANES), bf16),
+            pltpu.VMEM((n_seq, per_peer, q_width + LANES), bf16),
             pltpu.VMEM((requests, turns, q_width), bf16),
             pltpu.VMEM((tokens, q_width), f32),
             pltpu.VMEM((tokens, LANES), f32),
-            dma((9,)),
-            dma((n_seq, KV_HEADS)),
-            dma((n_seq, KV_HEADS)),
-            dma((n_seq, KV_HEADS)),
-            dma((n_seq, KV_HEADS)),
-            dma((n_seq,)),
-            dma((n_seq,)),
+            dma((8 + KV_HEADS,)),
+            dma((2,)),
+            dma((units, KV_HEADS)),
+            dma((KV_HEADS,)),
             dma((3,)),
             dma((3,)),
         ],

time: 21.3 us -> 19.8 us (0.930)
  Pallas kernels: 20.3 us -> 18.7 us
    pallas_call x1, Pallas kernels: 20.3 us -> 18.7 us  [local(): pl.pallas_call(functools.partial(kernel, n_seq, cap), out_shape=pltpu.VME...]
where the time goes in v1:
time: 19.8 us; the launch traced here: 19.6 us
  Pallas kernels  18.7 us (94%)
  local copies, waits for them, and re-layouts  0.89 us (4%)
    pallas_call x1, Pallas kernels, local(): pl.pallas_call(functools.partial(kernel, n_seq, cap), out_shape=pltpu.VME...  18.7 us
    reshape x1, local copies, waits for them, and re-layouts, local(): return served.reshape(1, requests, turns, q_width)  0.89 us

profile of v1, /device:TPU:1, one launch (start us, length us, event | category | flops | bytes accessed | tf_op | source)
XLA Modules:
  0.0 19.6 jit_solution(9924391068888901616)
XLA Ops:
  0.0 18.7 %shard_map.91 = bf16[32,4096]{1,0:T(8,128)(2,1)S(1)} custom-call(s32[16]{0:T(128)} %bitcast.7, s32[16]{0:T(128)} %parent_id_hbm.1, s32[16]{0:T(128)} %suffix_len_hbm.1, s32[2,16]{1,0:T(2,128)} %bitcast.6, s32[2,16]{1,0:T(2,128)} %parent_pages_hbm.1, s32[2]{0:T(128)} %parent_len_hbm.1, bf16[16,2,4096]{2,1,0:T(2,128)(2,1)} %bitcast.5, ...), custom_call_target="tpu_custom_call" | custom-call | tf_op jit(solution)/shard_map/pallas_call | solution.py:537
  18.7 0.9 %reshape.7 = bf16[1,16,2,4096]{3,2,1,0:T(2,128)(2,1)} reshape(bf16[32,4096]{1,0:T(8,128)(2,1)S(1)} %shard_map.91) | data formatting | bytes 524288 | tf_op jit(solution)/shard_map/reshape | solution.py:587

commit v2 on v1

--- a/solution.py
+++ b/solution.py
@@ -86,7 +86,8 @@
     heads_all = KV_HEADS * GROUP
     group_width = GROUP * HEAD_DIM
     half = LANES // 2
-    unit = min(4, n_seq)
+    quad = min(4, n_seq)
+    my_quad = me // quad * quad
     bits = [(me // 2**b) % 2 for b in range(n_seq.bit_length() - 1)]
 
     def peer_at(step):
@@ -180,7 +181,7 @@
             slots.at[peer, :, q_lanes(g)],
             arrived.at[me, :, q_lanes(g)],
             send_sem.at[0],
-            recv_sem.at[step // unit, g],
+            recv_sem.at[me // 2, g],
             {"seq": peer},
         )
 
@@ -391,19 +392,15 @@
         s_to_partner.wait_send()
         o_to_partner.wait_send()
 
-    batch = min(8, n_seq)
-
-    def answer(c, g, batch):
-        batch_rows = batch * per_peer
-        steps = [n_seq - 1 - batch * c - i for i in range(batch)]
-        peers = [peer_at(step) for step in steps]
-        rows = pl.ds(c * batch_rows, batch_rows)
-        for step in steps[::unit]:
-            if not isinstance(step, int):
-                pl.when(step // unit > 0)(lambda: slots_from(step // unit, g, unit).wait_recv())
-                pl.when(step // unit == 0)(lambda: slots_from(0, g, unit - 1).wait_recv())
+    def answer(first, count, g, mine):
+        peers = [first + i for i in range(count)]
+        rows = pl.ds(first * per_peer, count * per_peer)
+        for pair in [first // 2 + i for i in range(count // 2)]:
+            if mine:
+                pl.when(pair == me // 2)(lambda: slots_from(pair, g, 1).wait_recv())
+                pl.when(pair != me // 2)(lambda: slots_from(pair, g, 2).wait_recv())
             else:
-                slots_from(step // unit, g, unit if step >= unit else unit - 1).wait_recv()
+                slots_from(pair, g, 2).wait_recv()
 
         def gathered(first):
             return jnp.concatenate(
@@ -456,22 +453,27 @@
                     i * per_peer : (i + 1) * per_peer
                 ].astype(jnp.bfloat16)
 
-        for step, peer in zip(steps, peers):
-            if isinstance(step, int):
-                if step > 0:
-                    out_to(peer, g).start()
+        for peer in peers:
+            if mine:
+                pl.when(peer != me)(lambda: out_to(peer, g).start())
             else:
-                pl.when(step > 0)(lambda peer=peer: out_to(peer, g).start())
+                out_to(peer, g).start()
 
     @pl.when(on_decode)
     def _():
-        for g in range(KV_HEADS):
-            if n_seq == batch:
-                pieces = (1, 1, 1, 2)[g] if batch % 2 == 0 else 1
-                for c in range(pieces):
-                    answer(c, g, batch // pieces)
-            else:
-                each(0, n_seq // batch, lambda c: answer(c, g, batch))
+        if n_seq == 2 * quad == 8:
+            upper = me // quad
+            starts = [my_quad, 4 - 2 * upper, 6 - 6 * upper, 4 - 4 * upper]
+            for kind, g in [(3, 0), (0, 0), (3, 1), (0, 1), (3, 2), (0, 2), (2, 3), (1, 3), (0, 3)]:
+                answer(starts[kind], (4, 2, 2, 4)[kind], g, kind == 0)
+        else:
+            for g in range(KV_HEADS):
+                answer(my_quad, quad, g, True)
+                each(
+                    1,
+                    n_seq // quad,
+                    lambda i: answer(lax.rem(my_quad + i * quad, n_seq), quad, g, False),
+                )
 
     @pl.when(on_decode)
     def _():
@@ -490,10 +492,12 @@
             ).astype(jnp.bfloat16)
             return jnp.dot(pick_back, rows, preferred_element_type=jnp.float32)
 
-        for g in range(KV_HEADS):
+        last = KV_HEADS - 1
+        for g in range(last):
             out_from(g).wait_recv()
             for head in range(g * GROUP, (g + 1) * GROUP):
                 far_out[:, head * HEAD_DIM : (head + 1) * HEAD_DIM] = came(head * HEAD_DIM)
+        out_from(last).wait_recv()
         parts = came(q_width)
         far = (
             parts
@@ -507,8 +511,9 @@
         for head in range(heads_all):
             part = slice(head * HEAD_DIM, (head + 1) * HEAD_DIM)
             close = partner_o[:, part]
+            distant = came(head * HEAD_DIM) if head // GROUP == last else far_out[:, part]
             out_ref[:, part] = (
-                close + (far_out[:, part] - close) * far_share[:, head : head + 1]
+                close + (distant - close) * far_share[:, head : head + 1]
             ).astype(jnp.bfloat16)
         q_to_partner.wait_send()
         rows = pl.ds(0, n_seq - 1)
@@ -529,7 +534,6 @@
     tokens = requests * turns
     cap = max(4, 2 * requests // n_seq)
     per_peer = 2 * cap
-    units = n_seq // min(4, n_seq)
     bf16, f32 = jnp.bfloat16, jnp.float32
     vmem = pl.BlockSpec(memory_space=pltpu.VMEM)
     hbm = pl.BlockSpec(memory_space=pl.ANY)
@@ -565,7 +569,7 @@
             pltpu.VMEM((tokens, LANES), f32),
             dma((8 + KV_HEADS,)),
             dma((2,)),
-            dma((units, KV_HEADS)),
+            dma((n_seq // 2, KV_HEADS)),
             dma((KV_HEADS,)),
             dma((3,)),
             dma((3,)),

time: 19.8 us -> 19.2 us (0.970)
  Pallas kernels: 18.7 us -> 18.2 us
    pallas_call x1, Pallas kernels: 18.7 us -> 18.2 us  [local(): pl.pallas_call(functools.partial(kernel, n_seq, cap), out_shape=pltpu.VME...]
where the time goes in v2:
time: 19.2 us; the launch traced here: 19.1 us
  Pallas kernels  18.2 us (95%)
  local copies, waits for them, and re-layouts  0.89 us (5%)
    pallas_call x1, Pallas kernels, local(): pl.pallas_call(functools.partial(kernel, n_seq, cap), out_shape=pltpu.VME...  18.2 us
    reshape x1, local copies, waits for them, and re-layouts, local(): return served.reshape(1, requests, turns, q_width)  0.89 us

profile of v2, /device:TPU:1, one launch (start us, length us, event | category | flops | bytes accessed | tf_op | source)
XLA Modules:
  0.0 19.1 jit_solution(15664643156010631758)
XLA Ops:
  0.0 18.2 %shard_map.91 = bf16[32,4096]{1,0:T(8,128)(2,1)S(1)} custom-call(s32[16]{0:T(128)} %bitcast.7, s32[16]{0:T(128)} %parent_id_hbm.1, s32[16]{0:T(128)} %suffix_len_hbm.1, s32[2,16]{1,0:T(2,128)} %bitcast.6, s32[2,16]{1,0:T(2,128)} %parent_pages_hbm.1, s32[2]{0:T(128)} %parent_len_hbm.1, bf16[16,2,4096]{2,1,0:T(2,128)(2,1)} %bitcast.5, ...), custom_call_target="tpu_custom_call" | custom-call | tf_op jit(solution)/shard_map/pallas_call | solution.py:541
  18.2 0.9 %reshape.7 = bf16[1,16,2,4096]{3,2,1,0:T(2,128)(2,1)} reshape(bf16[32,4096]{1,0:T(8,128)(2,1)S(1)} %shard_map.91) | data formatting | bytes 524288 | tf_op jit(solution)/shard_map/reshape | solution.py:591

commit v3 on v2

--- a/solution.py
+++ b/solution.py
@@ -58,12 +58,10 @@
     slot_stat,
     far_out,
     near_send,
-    near_stat_send,
     ret_send,
     ret,
     partner_q,
     partner_o,
-    partner_stat,
     load_sem,
     send_sem,
     recv_sem,
@@ -140,9 +138,9 @@
 
     load_q = [
         pltpu.make_async_copy(
-            q_hbm.at[:, :, out_lanes(g)], q_ref.at[:, :, out_lanes(g)], load_sem.at[8 + g]
-        )
-        for g in range(KV_HEADS)
+            q_hbm.at[:, :, lanes], q_ref.at[:, :, lanes], load_sem.at[8 + i]
+        )
+        for i, lanes in enumerate((slice(0, group_width), slice(group_width, q_width)))
     ]
     for table in tables[:2]:
         table.start()
@@ -165,7 +163,6 @@
 
     q_to_partner = remote(q_ref, partner_q, psend_sem.at[0], precv_sem.at[0], partner)
     o_to_partner = remote(near_send, partner_o, psend_sem.at[1], precv_sem.at[1], partner)
-    s_to_partner = remote(near_stat_send, partner_stat, psend_sem.at[2], precv_sem.at[2], partner)
 
     def q_lanes(g):
         first = 0 if g == 0 else LANES + g * group_width
@@ -181,7 +178,7 @@
             slots.at[peer, :, q_lanes(g)],
             arrived.at[me, :, q_lanes(g)],
             send_sem.at[0],
-            recv_sem.at[me // 2, g],
+            recv_sem.at[me // quad, g],
             {"seq": peer},
         )
 
@@ -239,7 +236,8 @@
             )
         block_lanes = 4 * LANES
         for g in range(KV_HEADS):
-            load_q[g].wait()
+            if g < len(load_q):
+                load_q[g].wait()
             for c in range(group_width // block_lanes):
                 first = g * group_width + c * block_lanes
                 part = jnp.dot(
@@ -379,9 +377,8 @@
             for h, head in enumerate(heads):
                 keep(head, mixed[h])
             stat = stat + record(g, top, total)
-        near_stat_send[...] = log_sum(stat)
+        near_send[:, q_width:] = log_sum(stat)
         o_to_partner.start()
-        s_to_partner.start()
         bias = bias_of(request, length - 1 + turn)
         for g in range(KV_HEADS):
             heads = range(g * GROUP, (g + 1) * GROUP)
@@ -389,18 +386,12 @@
             mixed, _, _ = attend(g, query, bias)
             for h, head in enumerate(heads):
                 serve(head, mixed[h])
-        s_to_partner.wait_send()
         o_to_partner.wait_send()
 
     def answer(first, count, g, mine):
         peers = [first + i for i in range(count)]
         rows = pl.ds(first * per_peer, count * per_peer)
-        for pair in [first // 2 + i for i in range(count // 2)]:
-            if mine:
-                pl.when(pair == me // 2)(lambda: slots_from(pair, g, 1).wait_recv())
-                pl.when(pair != me // 2)(lambda: slots_from(pair, g, 2).wait_recv())
-            else:
-                slots_from(pair, g, 2).wait_recv()
+        slots_from(first // quad, g, quad - 1 if mine else quad).wait_recv()
 
         def gathered(first):
             return jnp.concatenate(
@@ -463,9 +454,9 @@
     def _():
         if n_seq == 2 * quad == 8:
             upper = me // quad
-            starts = [my_quad, 4 - 2 * upper, 6 - 6 * upper, 4 - 4 * upper]
-            for kind, g in [(3, 0), (0, 0), (3, 1), (0, 1), (3, 2), (0, 2), (2, 3), (1, 3), (0, 3)]:
-                answer(starts[kind], (4, 2, 2, 4)[kind], g, kind == 0)
+            for g in range(KV_HEADS):
+                answer(quad - quad * upper, quad, g, False)
+                answer(my_quad, quad, g, True)
         else:
             for g in range(KV_HEADS):
                 answer(my_quad, quad, g, True)
@@ -482,7 +473,6 @@
         target = 2 * spread(tok >> 1, places) + (tok & 1)
         unpick = jnp.where(iota((tokens, slot_rows), 1) == target, 1.0, 0.0)
         o_to_partner.wait_recv()
-        s_to_partner.wait_recv()
         pick_back = unpick.astype(jnp.bfloat16)
 
         def came(first):
@@ -504,7 +494,7 @@
             + pltpu.roll(parts, LANES - heads_all, 1)
             + pltpu.roll(parts, LANES - 2 * heads_all, 1)
         )
-        near = partner_stat[...]
+        near = partner_o[:, q_width:]
         top = jnp.maximum(far, near)
         far_weight = jnp.exp(far - top)
         far_share = far_weight / (far_weight + jnp.exp(near - top))
@@ -560,19 +550,17 @@
             pltpu.VMEM((n_seq * per_peer, page_store.shape[0]), f32),
             pltpu.VMEM((n_seq * per_peer, LANES), f32),
             pltpu.VMEM((tokens, q_width), f32),
-            pltpu.VMEM((tokens, q_width), f32),
-            pltpu.VMEM((tokens, LANES), f32),
+            pltpu.VMEM((tokens, q_width + LANES), f32),
             pltpu.VMEM((n_seq, per_peer, q_width + LANES), bf16),
             pltpu.VMEM((n_seq, per_peer, q_width + LANES), bf16),
             pltpu.VMEM((requests, turns, q_width), bf16),
-            pltpu.VMEM((tokens, q_width), f32),
-            pltpu.VMEM((tokens, LANES), f32),
-            dma((8 + KV_HEADS,)),
+            pltpu.VMEM((tokens, q_width + LANES), f32),
+            dma((10,)),
             dma((2,)),
-            dma((n_seq // 2, KV_HEADS)),
+            dma((n_seq // min(4, n_seq), KV_HEADS)),
             dma((KV_HEADS,)),
-            dma((3,)),
-            dma((3,)),
+            dma((2,)),
+            dma((2,)),
         ],
         compiler_params=pltpu.CompilerParams(
             collective_id=0, has_side_effects=True, vmem_limit_bytes=60 * 1024 * 1024

time: 19.2 us -> 18.7 us (0.974)
  Pallas kernels: 18.2 us -> 17.7 us
    pallas_call x1, Pallas kernels: 18.2 us -> 17.7 us  [local(): pl.pallas_call(functools.partial(kernel, n_seq, cap), out_shape=pltpu.VME...]
where the time goes in v3:
time: 18.7 us; the launch traced here: 18.6 us
  Pallas kernels  17.7 us (95%)
  local copies, waits for them, and re-layouts  0.89 us (5%)
    pallas_call x1, Pallas kernels, local(): pl.pallas_call(functools.partial(kernel, n_seq, cap), out_shape=pltpu.VME...  17.7 us
    reshape x1, local copies, waits for them, and re-layouts, local(): return served.reshape(1, requests, turns, q_width)  0.89 us

profile of v3, /device:TPU:1, one launch (start us, length us, event | category | flops | bytes accessed | tf_op | source)
XLA Modules:
  0.0 18.6 jit_solution(17435552124487038230)
XLA Ops:
  0.0 17.7 %shard_map.91 = bf16[32,4096]{1,0:T(8,128)(2,1)S(1)} custom-call(s32[16]{0:T(128)} %bitcast.7, s32[16]{0:T(128)} %parent_id_hbm.1, s32[16]{0:T(128)} %suffix_len_hbm.1, s32[2,16]{1,0:T(2,128)} %bitcast.6, s32[2,16]{1,0:T(2,128)} %parent_pages_hbm.1, s32[2]{0:T(128)} %parent_len_hbm.1, bf16[16,2,4096]{2,1,0:T(2,128)(2,1)} %bitcast.5, ...), custom_call_target="tpu_custom_call" | custom-call | tf_op jit(solution)/shard_map/pallas_call | solution.py:531
  17.7 0.9 %reshape.7 = bf16[1,16,2,4096]{3,2,1,0:T(2,128)(2,1)} reshape(bf16[32,4096]{1,0:T(8,128)(2,1)S(1)} %shard_map.91) | data formatting | bytes 524288 | tf_op jit(solution)/shard_map/reshape | solution.py:579

commit v4 on v3

--- a/solution.py
+++ b/solution.py
@@ -444,10 +444,11 @@
                     i * per_peer : (i + 1) * per_peer
                 ].astype(jnp.bfloat16)
 
-        for peer in peers:
-            if mine:
-                pl.when(peer != me)(lambda: out_to(peer, g).start())
-            else:
+        if mine:
+            for step in range(quad - 1, 0, -1):
+                out_to(peer_at(step), g).start()
+        else:
+            for peer in peers:
                 out_to(peer, g).start()
 
     @pl.when(on_decode)

time: 18.7 us -> 18.7 us (level)
  no operation moved by 1% of the time
where the time goes in v4:
time: 18.7 us; the launch traced here: 18.6 us
  Pallas kernels  17.7 us (95%)
  local copies, waits for them, and re-layouts  0.89 us (5%)
    pallas_call x1, Pallas kernels, local(): pl.pallas_call(functools.partial(kernel, n_seq, cap), out_shape=pltpu.VME...  17.7 us
    reshape x1, local copies, waits for them, and re-layouts, local(): return served.reshape(1, requests, turns, q_width)  0.89 us

profile of v4, /device:TPU:1, one launch (start us, length us, event | category | flops | bytes accessed | tf_op | source)
XLA Modules:
  0.0 18.6 jit_solution(2254230579343635653)
XLA Ops:
  0.0 17.7 %shard_map.91 = bf16[32,4096]{1,0:T(8,128)(2,1)S(1)} custom-call(s32[16]{0:T(128)} %bitcast.7, s32[16]{0:T(128)} %parent_id_hbm.1, s32[16]{0:T(128)} %suffix_len_hbm.1, s32[2,16]{1,0:T(2,128)} %bitcast.6, s32[2,16]{1,0:T(2,128)} %parent_pages_hbm.1, s32[2]{0:T(128)} %parent_len_hbm.1, bf16[16,2,4096]{2,1,0:T(2,128)(2,1)} %bitcast.5, ...), custom_call_target="tpu_custom_call" | custom-call | tf_op jit(solution)/shard_map/pallas_call | solution.py:532
  17.7 0.9 %reshape.7 = bf16[1,16,2,4096]{3,2,1,0:T(2,128)(2,1)} reshape(bf16[32,4096]{1,0:T(8,128)(2,1)S(1)} %shard_map.91) | data formatting | bytes 524288 | tf_op jit(solution)/shard_map/reshape | solution.py:580
